TPU v7x, 256 devices: a whole 4x4x8 slice. The times are simulated.
256 devices in a mesh: tm: 16 (over z, core), space: 16 (over y, x).
Axes of the slice: x: 4, y: 4, z: 8, core: 2. Of those that a mesh axis runs over, the one named last changes fastest.
Arguments:
- queries: bfloat16 [16, 2048, 48, 128], P('tm', 'space'), may hold values from -14 to 14
- noisy_keys: bfloat16 [16, 2048, 48, 128], P('tm', 'space'), may hold values from -14 to 14
- noisy_values: bfloat16 [16, 2048, 48, 128], P('tm', 'space'), may hold values from -6 to 6
- cache_keys: bfloat16 [16, 2048, 48, 128], P('tm', 'space'), may hold values from -12 to 12
- cache_values: bfloat16 [16, 2048, 48, 128], P('tm', 'space'), may hold values from -6 to 6
- block_list: int32 [16, 16, 12], P('tm'), may hold values from 0 to 63, as said below
- block_count: int32 [16, 16], P('tm'), may hold values from 1 to 12
- valid_tokens: int32 [16], replicated, may hold values from 1921 to 2048
Outputs:
- attended: bfloat16 [16, 2048, 48, 128], P('tm', 'space')
Inputs may be any that keep to these rules, and one draw needn't show every extreme that they name: `block_list`: entries index the 64 key blocks of stretch c's window in order of offset, the last 16 being stretch c's own blocks. The first block_count[c, a] entries are distinct and name only blocks of stretches 0 or later; the first of them is query block a's own block; later entries repeat that own block.
All inputs are finite; a program needn't handle non-finite values.
Results may differ from a plain program's by a relative error of at most 0.0035.
Values may be sent and summed in bfloat16 or wider, within the bound.
No kernel may reach another device: no remote copies, remote signals or barrier semaphores. Data moves between devices by JAX's collectives and lax.ppermute only.
A program may use at most 128 MiB of HBM per device.

v0:
```python
import math
import jax
import jax.numpy as jnp
from jax import lax
from jax.sharding import PartitionSpec as P

BLOCK = 128
WIN = 4
LIST = 12
NEG = -1e30


def passed_along(block, axis, distance):
    devices = range(lax.axis_size(axis))
    route = [(i - distance, i) for i in devices if i - distance in devices]
    return lax.ppermute(block, axis, route)


def hand_forward(pair):
    earlier = []
    carried = pair
    for distance in range(1, WIN):
        carried = passed_along(carried, "tm", 1)
        earlier.append(carried)
    return earlier


def on_device(
    queries,
    noisy_keys,
    noisy_values,
    cache_keys,
    cache_values,
    block_list,
    block_count,
    valid_tokens,
):
    stretch_now = lax.axis_index("tm")
    fresh = jnp.concatenate((queries, noisy_keys, noisy_values), 0)
    fresh = lax.all_to_all(fresh, "space", split_axis=2, concat_axis=1, tiled=True)
    own_cache = jnp.concatenate((cache_keys, cache_values), 0)
    earlier = hand_forward(own_cache)
    stacked = jnp.stack(earlier[::-1], 0)
    past = lax.all_to_all(stacked, "space", split_axis=3, concat_axis=2, tiled=True)
    stretch_len = fresh.shape[1]
    local_heads = fresh.shape[2]
    head_size = fresh.shape[3]
    block_total = stretch_len // BLOCK
    fresh_heads = jnp.transpose(fresh, (0, 2, 1, 3))
    past_heads = jnp.transpose(past, (1, 3, 0, 2, 4))
    window_keys = jnp.concatenate((past_heads[0], fresh_heads[1][:, None]), 1)
    window_values = jnp.concatenate((past_heads[1], fresh_heads[2][:, None]), 1)
    query_blocks = fresh_heads[0].reshape(local_heads, block_total, BLOCK, head_size)
    key_blocks = window_keys.reshape(local_heads, WIN * block_total, BLOCK, head_size)
    value_blocks = window_values.reshape(local_heads, WIN * block_total, BLOCK, head_size)
    positions = jnp.arange(stretch_len)
    sources = stretch_now - (WIN - 1) + jnp.arange(WIN)
    lengths = valid_tokens[jnp.clip(sources, 0, valid_tokens.shape[0] - 1)]
    key_live = ((sources[:, None] >= 0) & (positions[None, :] < lengths[:, None])).reshape(
        WIN * block_total, BLOCK
    )
    stretch_lists = block_list[0]
    stretch_counts = block_count[0]
    score_scale = 1.0 / math.sqrt(head_size)
    start_best = jnp.full((local_heads, block_total, BLOCK), NEG, jnp.float32)
    start_total = jnp.zeros((local_heads, block_total, BLOCK), jnp.float32)
    start_accum = jnp.zeros((local_heads, block_total, BLOCK, head_size), jnp.float32)

    def slot_step(slot_index, carry):
        row_best, row_total, accum = carry
        chosen = lax.dynamic_slice_in_dim(stretch_lists, slot_index, 1, 1)[:, 0]
        keys_here = key_blocks[:, chosen]
        values_here = value_blocks[:, chosen]
        scores = (
            jnp.einsum(
                "haqd,hakd->haqk", query_blocks, keys_here, preferred_element_type=jnp.float32
            )
            * score_scale
        )
        allowed = (slot_index < stretch_counts)[None, :, None, None] & key_live[chosen][
            None, :, None, :
        ]
        scores = jnp.where(allowed, scores, NEG)
        new_best = jnp.maximum(row_best, jnp.max(scores, axis=-1))
        weights = jnp.where(allowed, jnp.exp(scores - new_best[..., None]), 0.0)
        shrink = jnp.exp(row_best - new_best)
        row_total = row_total * shrink + jnp.sum(weights, axis=-1)
        pieces = jnp.einsum(
            "haqk,hakd->haqd",
            weights.astype(jnp.bfloat16),
            values_here,
            preferred_element_type=jnp.float32,
        )
        accum = accum * shrink[..., None] + pieces
        return (new_best, row_total, accum)

    row_best, row_total, accum = lax.fori_loop(
        0, LIST, slot_step, (start_best, start_total, start_accum)
    )
    mixed_rows = accum / row_total[..., None]
    mixed_rows = mixed_rows.reshape(local_heads, stretch_len, head_size)
    query_live = positions < valid_tokens[stretch_now]
    masked = jnp.where(query_live[None, :, None], mixed_rows, 0.0).astype(jnp.bfloat16)
    attended_local = jnp.transpose(masked, (1, 0, 2))
    return lax.all_to_all(attended_local[None], "space", split_axis=1, concat_axis=2, tiled=True)


def solution(mesh):
    placed = (
        P("tm", "space", None, None),
        P("tm", "space", None, None),
        P("tm", "space", None, None),
        P("tm", "space", None, None),
        P("tm", "space", None, None),
        P("tm", None, None),
        P("tm", None),
        P(),
    )
    return jax.shard_map(
        on_device,
        mesh=mesh,
        in_specs=placed,
        out_specs=P("tm", "space", None, None),
        check_vma=False,
    )
```

profile of v0, /device:TPU:192, one launch (start us, length us, event | category | flops | bytes accessed | tf_op | source)
XLA Modules:
  0.0 597.0 jit_solution(18413690183494990930)
XLA Ops:
  4.9 36.7 %collective-permute-done = bf16[2,128,48,128]{3,1,0,2:T(8,128)(2,1)S(1)} collective-permute-done((bf16[2,128,48,128]{3,1,0,2:T(8,128)(2,1)S(1)}, bf16[2,128,48,128]{3,1,0,2:T(8,128)(2,1)S(1)}, u32[]{:S(2)}, u32[]{:S(2)}) %collective-permute-start) | collective-permute-done | bytes 3145760 | tf_op jit(solution)/shard_map/ppermute | solution.py:16
  47.2 7.1 %all-to-all-start.1 = ((bf16[3,128,48,128]{3,1,0,2:T(8,128)(2,1)}), bf16[3,128,48,128]{3,1,0,2:T(8,128)(2,1)}, u32[]{:S(2)}, u32[]{:S(2)}) async-start(bf16[3,128,48,128]{3,1,0,2:T(8,128)(2,1)} %pad_maximum_fusion.3), calls=%async_computation.1 | async-start | bytes 9437184 | tf_op jit(solution)/shard_map/all_to_all | solution.py:40
  54.3 25.9 %collective-permute-done.1 = bf16[2,128,48,128]{3,1,0,2:T(8,128)(2,1)} collective-permute-done((bf16[2,128,48,128]{3,1,0,2:T(8,128)(2,1)S(1)}, bf16[2,128,48,128]{3,1,0,2:T(8,128)(2,1)}, u32[]{:S(2)}, u32[]{:S(2)}) %collective-permute-start.1) | collective-permute-done | bytes 3145760 | tf_op jit(solution)/shard_map/ppermute | solution.py:16
  82.2 36.9 %collective-permute-done.2 = bf16[2,128,48,128]{3,1,0,2:T(8,128)(2,1)S(1)} collective-permute-done((bf16[2,128,48,128]{3,1,0,2:T(8,128)(2,1)}, bf16[2,128,48,128]{3,1,0,2:T(8,128)(2,1)S(1)}, u32[]{:S(2)}, u32[]{:S(2)}) %collective-permute-start.2) | collective-permute-done | bytes 3145760 | tf_op jit(solution)/shard_map/ppermute | solution.py:16
  119.0 6.3 %pad_maximum_fusion = bf16[3,2,128,48,128]{4,2,1,0,3:T(8,128)(2,1)} fusion(bf16[1,2,128,48,128]{4,2,1,0,3:T(8,128)(2,1)S(1)} %bitcast.98, bf16[1,2,128,48,128]{4,2,1,0,3:T(8,128)(2,1)} %bitcast.5, bf16[1,2,128,48,128]{4,2,1,0,3:T(8,128)(2,1)S(1)} %bitcast.99), kind=kLoop, calls=%fused_computation.37 | loop fusion | flops 9437184 | bytes 18874368 | tf_op jit(solution)/shard_map/stack | solution.py:43
  125.4 3.4 all-to-all-done.1
  128.8 5.0 all-to-all-start
  136.1 3.3 copy.65
  141.3 133.8 %all-to-all-done = bf16[3,2,128,48,128]{4,2,1,0,3:T(8,128)(2,1)} async-done(((bf16[3,2,128,48,128]{4,2,1,0,3:T(8,128)(2,1)}), bf16[3,2,128,48,128]{4,2,1,0,3:T(8,128)(2,1)}, u32[]{:S(2)}, u32[]{:S(2)}) %all-to-all-start) | async-done | bytes 9437216 | tf_op jit(solution)/shard_map/all_to_all | solution.py:44
  275.2 11.6 %copy.60 = bf16[3,2,16,128,3,128]{5,3,2,4,1,0:T(8,128)(2,1)} copy(bf16[3,2,16,128,3,128]{5,3,1,0,4,2:T(8,128)(2,1)} %bitcast.9) | data formatting | bytes 18874368 | tf_op jit(solution)/shard_map/all_to_all | solution.py:44
  286.8 6.6 %slice_bitcast_fusion = (bf16[3,3,2048,128]{3,2,0,1:T(8,128)(2,1)S(1)}, bf16[3,3,2048,128]{3,2,0,1:T(8,128)(2,1)}) fusion(bf16[2,3,3,2048,128]{4,3,1,0,2:T(8,128)(2,1)} %bitcast.91), kind=kLoop, calls=%fused_computation.40 | loop fusion | bytes 18874368 | tf_op jit(solution)/shard_map/squeeze | solution.py:52
  293.4 4.0 pad_maximum_fusion.1
  300.5 3.1 copy.67
  303.6 247.9 %while.18 = (s32[]{:T(128)}, f32[3,16,128]{2,1,0:T(8,128)S(1)}, f32[3,16,128]{2,1,0:T(8,128)S(1)}, f32[3,16,128,128]{3,2,1,0:T(8,128)}, s32[16]{0:T(128)S(1)}, /...) while((s32[]{:T(128)}, f32[3,16,128]{2,1,0:T(8,128)S(1)}, ...), condition=%wide.region_3.4_spmd.clone, body=%wide.region_0.3_spmd.clone.sunk | while | flops 415286336 | bytes 27167672 | solution.py:97
  304.4 4.7 gather_fusion.1
  309.1 4.1 bitcast_reduce_fusion.2
  314.4 4.7 gather_fusion.2
  319.1 4.7 fusion.47
  324.6 4.7 gather_fusion.1
  329.3 4.1 bitcast_reduce_fusion.2
  334.6 4.7 gather_fusion.2
  339.3 5.2 fusion.47
  345.3 4.7 gather_fusion.1
  350.0 4.1 bitcast_reduce_fusion.2
  355.3 4.7 gather_fusion.2
  360.0 5.2 fusion.47
  366.0 4.7 gather_fusion.1
  370.7 4.1 bitcast_reduce_fusion.2
  376.0 4.7 gather_fusion.2
  380.7 5.2 fusion.47
  386.7 4.7 gather_fusion.1
  391.4 4.1 bitcast_reduce_fusion.2
  396.7 4.7 gather_fusion.2
  401.4 5.2 fusion.47
  407.4 4.7 gather_fusion.1
  412.1 4.1 bitcast_reduce_fusion.2
  417.4 4.7 gather_fusion.2
  422.1 5.2 fusion.47
  428.1 4.7 gather_fusion.1
  432.8 4.1 bitcast_reduce_fusion.2
  438.1 4.7 gather_fusion.2
  442.8 5.2 fusion.47
  448.8 4.7 gather_fusion.1
  453.5 4.1 bitcast_reduce_fusion.2
  458.8 4.7 gather_fusion.2
  463.5 5.2 fusion.47
  469.5 4.7 gather_fusion.1
  474.2 4.1 bitcast_reduce_fusion.2
  479.5 4.7 gather_fusion.2
  484.2 5.2 fusion.47
  490.2 4.7 gather_fusion.1
  494.9 4.1 bitcast_reduce_fusion.2
  500.2 4.7 gather_fusion.2
  504.9 5.2 fusion.47
  510.9 4.7 gather_fusion.1
  515.6 4.1 bitcast_reduce_fusion.2
  520.9 4.7 gather_fusion.2
  525.6 5.2 fusion.47
  531.6 4.7 gather_fusion.1
  536.3 4.1 bitcast_reduce_fusion.2
  541.6 4.7 gather_fusion.2
  546.3 5.2 fusion.47
  555.3 7.5 %fusion.23 = bf16[3,2048,128]{2,0,1:T(4,128)(2,1)S(1)} fusion(bf16[3,16,128,128]{3,0,2,1:T(4,128)(2,1)S(1)} %copy.68, pred[2048]{0:T(1024)(128)(4,1)S(1)} %iota_compare_fusion), kind=kLoop, calls=%fused_computation.44 | loop fusion | flops 786432 | bytes 3147776 | tf_op jit(solution)/shard_map/convert_element_type | solution.py:103
  562.8 31.7 %all_to_all.54 = bf16[1,2048,3,128]{3,2,0,1:T(4,128)(2,1)S(1)} all-to-all(bf16[1,2048,3,128]{3,2,0,1:T(4,128)(2,1)S(1)} %bitcast.95), channel_id=1, replica_groups=mesh['tm'=16,'space'=16] {'space'}, dimensions={1} | all-to-all | bytes 3145728 | tf_op jit(solution)/shard_map/all_to_all | solution.py:105
  (166 shorter events, 48.9 us)
Async XLA Ops:
  0.0 1.9 copy-start.1
  2.4 41.1 %copy-start.2 = (bf16[1,128,48,128]{3,2,1,0:T(8,128)(2,1)S(1)}, bf16[1,128,48,128]{3,2,1,0:T(8,128)(2,1)}, u32[]{:S(2)}) copy-start(bf16[1,128,48,128]{3,2,1,0:T(8,128)(2,1)} %param.10) | copy-start | bytes 4718596
  2.7 41.2 %copy-start.3 = (bf16[1,128,48,128]{3,2,1,0:T(8,128)(2,1)S(1)}, bf16[1,128,48,128]{3,2,1,0:T(8,128)(2,1)}, u32[]{:S(2)}) copy-start(bf16[1,128,48,128]{3,2,1,0:T(8,128)(2,1)} %param.11) | copy-start | bytes 4718596
  2.7 41.6 %copy-start.4 = (bf16[1,128,48,128]{3,2,1,0:T(8,128)(2,1)S(1)}, bf16[1,128,48,128]{3,2,1,0:T(8,128)(2,1)}, u32[]{:S(2)}) copy-start(bf16[1,128,48,128]{3,2,1,0:T(8,128)(2,1)} %param.12) | copy-start | bytes 4718596
  2.7 38.9 %collective-permute-start = (bf16[2,128,48,128]{3,1,0,2:T(8,128)(2,1)S(1)}, bf16[2,128,48,128]{3,1,0,2:T(8,128)(2,1)S(1)}, u32[]{:S(2)}, u32[]{:S(2)}) collective-permute-start(bf16[2,128,48,128]{3,1,0,2:T(8,128)(2,1)S(1)} %pad_maximum_fusion.4), channel_id=1, source_target_pairs={{0,16},{16,32},{32,48},{48,64},{64,80},{80,96},{96,112},{112,128},... | collective-permute-start | bytes 9437192 | tf_op jit(solution)/shard_map/ppermute | solution.py:16
  41.6 38.7 %collective-permute-start.1 = (bf16[2,128,48,128]{3,1,0,2:T(8,128)(2,1)S(1)}, bf16[2,128,48,128]{3,1,0,2:T(8,128)(2,1)}, u32[]{:S(2)}, u32[]{:S(2)}) collective-permute-start(bf16[2,128,48,128]{3,1,0,2:T(8,128)(2,1)S(1)} %collective-permute-done), channel_id=1, source_target_pairs={{0,16},{16,32},{32,48},{48,64},{64,80},{80,96},{96,112},{112,128},... | collective-permute-start | bytes 9437192 | tf_op jit(solution)/shard_map/ppermute | solution.py:16
  47.2 81.5 %all-to-all-start.1 = ((bf16[3,128,48,128]{3,1,0,2:T(8,128)(2,1)}), bf16[3,128,48,128]{3,1,0,2:T(8,128)(2,1)}, u32[]{:S(2)}, u32[]{:S(2)}) async-start(bf16[3,128,48,128]{3,1,0,2:T(8,128)(2,1)} %pad_maximum_fusion.3), calls=%async_computation.1 | async-start | bytes 9437184 | tf_op jit(solution)/shard_map/all_to_all | solution.py:40
  80.2 38.8 %collective-permute-start.2 = (bf16[2,128,48,128]{3,1,0,2:T(8,128)(2,1)}, bf16[2,128,48,128]{3,1,0,2:T(8,128)(2,1)S(1)}, u32[]{:S(2)}, u32[]{:S(2)}) collective-permute-start(bf16[2,128,48,128]{3,1,0,2:T(8,128)(2,1)} %collective-permute-done.1), channel_id=1, source_target_pairs={{0,16},{16,32},{32,48},{48,64},{64,80},{80,96},{96,112},{112,128},... | collective-permute-start | bytes 9437192 | tf_op jit(solution)/shard_map/ppermute | solution.py:16
  125.3 8.5 %copy-start = (s32[16]{0:T(128)S(1)}, s32[16]{0:T(128)}, u32[]{:S(2)}) copy-start(s32[16]{0:T(128)} %param.17) | copy-start | bytes 196
  125.3 9.4 %copy-start.5 = (s32[1,16,12]{1,0,2:T(1,128)S(1)}, s32[1,16,12]{1,0,2:T(1,128)}, u32[]{:S(2)}) copy-start(s32[1,16,12]{1,0,2:T(1,128)} %param.15) | copy-start | bytes 2308
  128.8 146.4 %all-to-all-start = ((bf16[3,2,128,48,128]{4,2,1,0,3:T(8,128)(2,1)}), bf16[3,2,128,48,128]{4,2,1,0,3:T(8,128)(2,1)}, u32[]{:S(2)}, u32[]{:S(2)}) async-start(bf16[3,2,128,48,128]{4,2,1,0,3:T(8,128)(2,1)} %pad_maximum_fusion), calls=%async_computation | async-start | bytes 18874368 | tf_op jit(solution)/shard_map/all_to_all | solution.py:44
  300.5 3.1 copy-start.6
where the time goes:
time: 599 us; the launch traced here: 597 us
  waiting for transfers between devices  237 us (40%)
  local copies, waits for them, and re-layouts  159 us (27%)
  matrix products  111 us (19%)
  other arithmetic  39.7 us (7%)
  blocking collectives  31.7 us (5%)
  starting transfers between devices  18.1 us (3%)
    all_to_all x1, waiting for transfers between devices, on_device(): lax.all_to_all(stacked, 'space', split_axis=3, concat_axis=2, tiled=True)  134 us
    ppermute x3, waiting for transfers between devices, passed_along(): return lax.ppermute(block, axis, route)  99.5 us
    dot_general x12, matrix products, slot_step(): jnp.einsum('haqk,hakd->haqd', weights.astype(jnp.bfloat16), values_here,...  62.2 us
    gather x12, local copies, waits for them, and re-layouts, slot_step(): keys_here = key_blocks[:, chosen]  56.5 us
    gather x12, local copies, waits for them, and re-layouts, slot_step(): values_here = value_blocks[:, chosen]  56.5 us
    dot_general x12, matrix products, slot_step(): jnp.einsum('haqd,hakd->haqk', query_blocks, keys_here, preferred_element_...  49.1 us
    all_to_all x1, blocking collectives, on_device(): lax.all_to_all(attended_local[None], 'space', split_axis=1, concat_axis=2...  31.7 us
    reduce_sum x12, other arithmetic, slot_step(): row_total = row_total * shrink + jnp.sum(weights, axis=-1)  13.6 us
  transfers between devices with their start and end apart: 5, of which 5 were waited for; matrix products, arithmetic and copies ran while one was open for 3% of the time, Pallas kernels for 0%

commit v1 on v0

--- a/solution.py
+++ b/solution.py
@@ -8,6 +8,12 @@
 WIN = 4
 LIST = 12
 NEG = -1e30
+
+
+def swap_blocks(x, mesh_axis, split, join):
+    shards = jnp.split(x, lax.axis_size(mesh_axis), axis=split)
+    received = lax.all_to_all(jnp.stack(shards), mesh_axis, 0, 0)
+    return jnp.concatenate(received, axis=join)
 
 
 def passed_along(block, axis, distance):
@@ -102,7 +108,7 @@
     query_live = positions < valid_tokens[stretch_now]
     masked = jnp.where(query_live[None, :, None], mixed_rows, 0.0).astype(jnp.bfloat16)
     attended_local = jnp.transpose(masked, (1, 0, 2))
-    return lax.all_to_all(attended_local[None], "space", split_axis=1, concat_axis=2, tiled=True)
+    return swap_blocks(attended_local[None], "space", 1, 2)
 
 
 def solution(mesh):

time: 599 us -> 586 us (0.978)
  other arithmetic: 39.7 us -> 32.9 us
    convert_element_type x1, other arithmetic: 7.49 us -> 0.69 us  [on_device(): jnp.where(query_live[None, :, None], mixed_rows, 0.0).astype(jnp.bfloat16)]
where the time goes in v1:
time: 586 us; the launch traced here: 584 us
  waiting for transfers between devices  237 us (40%)
  local copies, waits for them, and re-layouts  158 us (27%)
  matrix products  111 us (19%)
  other arithmetic  32.9 us (6%)
  blocking collectives  26 us (4%)
  starting transfers between devices  17.9 us (3%)
    all_to_all x1, waiting for transfers between devices, on_device(): lax.all_to_all(stacked, 'space', split_axis=3, concat_axis=2, tiled=True)  134 us
    ppermute x3, waiting for transfers between devices, passed_along(): return lax.ppermute(block, axis, route)  98.5 us
    dot_general x12, matrix products, slot_step(): jnp.einsum('haqk,hakd->haqd', weights.astype(jnp.bfloat16), values_here,...  62.2 us
    gather x12, local copies, waits for them, and re-layouts, slot_step(): keys_here = key_blocks[:, chosen]  56.5 us
    gather x12, local copies, waits for them, and re-layouts, slot_step(): values_here = value_blocks[:, chosen]  56.5 us
    dot_general x12, matrix products, slot_step(): jnp.einsum('haqd,hakd->haqk', query_blocks, keys_here, preferred_element_...  49.1 us
    all_to_all x1, blocking collectives, swap_blocks(): received = lax.all_to_all(jnp.stack(shards), mesh_axis, 0, 0)  26 us
    reduce_sum x12, other arithmetic, slot_step(): row_total = row_total * shrink + jnp.sum(weights, axis=-1)  13.6 us
  transfers between devices with their start and end apart: 5, of which 5 were waited for; matrix products, arithmetic and copies ran while one was open for 3% of the time, Pallas kernels for 0%

profile of v1, /device:TPU:192, one launch (start us, length us, event | category | flops | bytes accessed | tf_op | source)
XLA Modules:
  0.0 584.0 jit_solution(6617103241474957194)
XLA Ops:
  4.8 36.7 %collective-permute-done = bf16[2,128,48,128]{3,1,0,2:T(8,128)(2,1)S(1)} collective-permute-done((bf16[2,128,48,128]{3,1,0,2:T(8,128)(2,1)S(1)}, bf16[2,128,48,128]{3,1,0,2:T(8,128)(2,1)S(1)}, u32[]{:S(2)}, u32[]{:S(2)}) %collective-permute-start) | collective-permute-done | bytes 3145760 | tf_op jit(solution)/shard_map/ppermute | solution.py:22
  48.1 7.1 %all-to-all-start.1 = ((bf16[3,128,48,128]{3,1,0,2:T(8,128)(2,1)}), bf16[3,128,48,128]{3,1,0,2:T(8,128)(2,1)}, u32[]{:S(2)}, u32[]{:S(2)}) async-start(bf16[3,128,48,128]{3,1,0,2:T(8,128)(2,1)} %pad_maximum_fusion.3), calls=%async_computation.1 | async-start | bytes 9437184 | tf_op jit(solution)/shard_map/all_to_all | solution.py:46
  55.2 24.9 %collective-permute-done.1 = bf16[2,128,48,128]{3,1,0,2:T(8,128)(2,1)} collective-permute-done((bf16[2,128,48,128]{3,1,0,2:T(8,128)(2,1)S(1)}, bf16[2,128,48,128]{3,1,0,2:T(8,128)(2,1)}, u32[]{:S(2)}, u32[]{:S(2)}) %collective-permute-start.1) | collective-permute-done | bytes 3145760 | tf_op jit(solution)/shard_map/ppermute | solution.py:22
  82.0 36.9 %collective-permute-done.2 = bf16[2,128,48,128]{3,1,0,2:T(8,128)(2,1)S(1)} collective-permute-done((bf16[2,128,48,128]{3,1,0,2:T(8,128)(2,1)}, bf16[2,128,48,128]{3,1,0,2:T(8,128)(2,1)S(1)}, u32[]{:S(2)}, u32[]{:S(2)}) %collective-permute-start.2) | collective-permute-done | bytes 3145760 | tf_op jit(solution)/shard_map/ppermute | solution.py:22
  118.9 6.3 %pad_maximum_fusion = bf16[3,2,128,48,128]{4,2,1,0,3:T(8,128)(2,1)} fusion(bf16[1,2,128,48,128]{4,2,1,0,3:T(8,128)(2,1)S(1)} %bitcast.177, bf16[1,2,128,48,128]{4,2,1,0,3:T(8,128)(2,1)} %bitcast.5, bf16[1,2,128,48,128]{4,2,1,0,3:T(8,128)(2,1)S(1)} %bitcast.178), kind=kLoop, calls=%fused_computation.37 | loop fusion | flops 9437184 | bytes 18874368 | tf_op jit(solution)/shard_map/stack | solution.py:49
  125.2 4.4 all-to-all-done.1
  129.6 5.0 all-to-all-start
  136.9 3.3 copy.123
  142.2 133.8 %all-to-all-done = bf16[3,2,128,48,128]{4,2,1,0,3:T(8,128)(2,1)} async-done(((bf16[3,2,128,48,128]{4,2,1,0,3:T(8,128)(2,1)}), bf16[3,2,128,48,128]{4,2,1,0,3:T(8,128)(2,1)}, u32[]{:S(2)}, u32[]{:S(2)}) %all-to-all-start) | async-done | bytes 9437216 | tf_op jit(solution)/shard_map/all_to_all | solution.py:50
  276.0 11.6 %copy.118 = bf16[3,2,16,128,3,128]{5,3,2,4,1,0:T(8,128)(2,1)} copy(bf16[3,2,16,128,3,128]{5,3,1,0,4,2:T(8,128)(2,1)} %bitcast.9) | data formatting | bytes 18874368 | tf_op jit(solution)/shard_map/all_to_all | solution.py:50
  287.6 6.6 %slice_bitcast_fusion = (bf16[3,3,2048,128]{3,2,0,1:T(8,128)(2,1)S(1)}, bf16[3,3,2048,128]{3,2,0,1:T(8,128)(2,1)}) fusion(bf16[2,3,3,2048,128]{4,3,1,0,2:T(8,128)(2,1)} %bitcast.156), kind=kLoop, calls=%fused_computation.40 | loop fusion | bytes 18874368 | tf_op jit(solution)/shard_map/squeeze | solution.py:58
  294.2 4.0 pad_maximum_fusion.1
  298.3 3.1 copy.124
  301.4 3.1 copy.125
  304.5 247.9 %while.18 = (s32[]{:T(128)}, f32[3,16,128]{2,1,0:T(8,128)S(1)}, f32[3,16,128]{2,1,0:T(8,128)S(1)}, f32[3,16,128,128]{3,2,1,0:T(8,128)}, s32[16]{0:T(128)S(1)}, /...) while((s32[]{:T(128)}, f32[3,16,128]{2,1,0:T(8,128)S(1)}, ...), condition=%wide.region_3.4_spmd.clone, body=%wide.region_0.3_spmd.clone.sunk | while | flops 415286336 | bytes 27167672 | solution.py:103
  305.2 4.7 gather_fusion.1
  309.9 4.1 bitcast_reduce_fusion.2
  315.2 4.7 gather_fusion.2
  319.9 4.7 fusion.63
  325.4 4.7 gather_fusion.1
  330.1 4.1 bitcast_reduce_fusion.2
  335.4 4.7 gather_fusion.2
  340.1 5.2 fusion.63
  346.1 4.7 gather_fusion.1
  350.8 4.1 bitcast_reduce_fusion.2
  356.1 4.7 gather_fusion.2
  360.8 5.2 fusion.63
  366.8 4.7 gather_fusion.1
  371.5 4.1 bitcast_reduce_fusion.2
  376.8 4.7 gather_fusion.2
  381.5 5.2 fusion.63
  387.5 4.7 gather_fusion.1
  392.2 4.1 bitcast_reduce_fusion.2
  397.5 4.7 gather_fusion.2
  402.2 5.2 fusion.63
  408.2 4.7 gather_fusion.1
  412.9 4.1 bitcast_reduce_fusion.2
  418.2 4.7 gather_fusion.2
  422.9 5.2 fusion.63
  428.9 4.7 gather_fusion.1
  433.6 4.1 bitcast_reduce_fusion.2
  438.9 4.7 gather_fusion.2
  443.6 5.2 fusion.63
  449.6 4.7 gather_fusion.1
  454.3 4.1 bitcast_reduce_fusion.2
  459.6 4.7 gather_fusion.2
  464.3 5.2 fusion.63
  470.3 4.7 gather_fusion.1
  475.0 4.1 bitcast_reduce_fusion.2
  480.3 4.7 gather_fusion.2
  485.0 5.2 fusion.63
  491.0 4.7 gather_fusion.1
  495.8 4.1 bitcast_reduce_fusion.2
  501.0 4.7 gather_fusion.2
  505.7 5.2 fusion.63
  511.7 4.7 gather_fusion.1
  516.5 4.1 bitcast_reduce_fusion.2
  521.7 4.7 gather_fusion.2
  526.4 5.2 fusion.63
  532.4 4.7 gather_fusion.1
  537.2 4.1 bitcast_reduce_fusion.2
  542.4 4.7 gather_fusion.2
  547.1 5.2 fusion.63
  555.9 26.0 %all_to_all.41 = bf16[16,1,128,3,128]{4,2,3,1,0:T(8,128)(2,1)S(1)} all-to-all(bf16[16,1,128,3,128]{4,2,3,1,0:T(8,128)(2,1)S(1)} %fusion.24), channel_id=1, replica_groups=mesh['tm'=16,'space'=16] {'space'}, dimensions={0} | all-to-all | bytes 3145728 | tf_op jit(solution)/shard_map/all_to_all | solution.py:15
  (179 shorter events, 45.9 us)
Async XLA Ops:
  0.0 1.9 copy-start.1
  2.4 41.0 %copy-start.2 = (bf16[1,128,48,128]{3,2,1,0:T(8,128)(2,1)S(1)}, bf16[1,128,48,128]{3,2,1,0:T(8,128)(2,1)}, u32[]{:S(2)}) copy-start(bf16[1,128,48,128]{3,2,1,0:T(8,128)(2,1)} %param.10) | copy-start | bytes 4718596
  2.7 41.1 %copy-start.3 = (bf16[1,128,48,128]{3,2,1,0:T(8,128)(2,1)S(1)}, bf16[1,128,48,128]{3,2,1,0:T(8,128)(2,1)}, u32[]{:S(2)}) copy-start(bf16[1,128,48,128]{3,2,1,0:T(8,128)(2,1)} %param.11) | copy-start | bytes 4718596
  2.7 38.7 %collective-permute-start = (bf16[2,128,48,128]{3,1,0,2:T(8,128)(2,1)S(1)}, bf16[2,128,48,128]{3,1,0,2:T(8,128)(2,1)S(1)}, u32[]{:S(2)}, u32[]{:S(2)}) collective-permute-start(bf16[2,128,48,128]{3,1,0,2:T(8,128)(2,1)S(1)} %pad_maximum_fusion.4), channel_id=1, source_target_pairs={{0,16},{16,32},{32,48},{48,64},{64,80},{80,96},{96,112},{112,128},... | collective-permute-start | bytes 9437192 | tf_op jit(solution)/shard_map/ppermute | solution.py:22
  41.4 38.7 %collective-permute-start.1 = (bf16[2,128,48,128]{3,1,0,2:T(8,128)(2,1)S(1)}, bf16[2,128,48,128]{3,1,0,2:T(8,128)(2,1)}, u32[]{:S(2)}, u32[]{:S(2)}) collective-permute-start(bf16[2,128,48,128]{3,1,0,2:T(8,128)(2,1)S(1)} %collective-permute-done), channel_id=1, source_target_pairs={{0,16},{16,32},{32,48},{48,64},{64,80},{80,96},{96,112},{112,128},... | collective-permute-start | bytes 9437192 | tf_op jit(solution)/shard_map/ppermute | solution.py:22
  43.8 1.4 copy-start.4
  48.1 81.5 %all-to-all-start.1 = ((bf16[3,128,48,128]{3,1,0,2:T(8,128)(2,1)}), bf16[3,128,48,128]{3,1,0,2:T(8,128)(2,1)}, u32[]{:S(2)}, u32[]{:S(2)}) async-start(bf16[3,128,48,128]{3,1,0,2:T(8,128)(2,1)} %pad_maximum_fusion.3), calls=%async_computation.1 | async-start | bytes 9437184 | tf_op jit(solution)/shard_map/all_to_all | solution.py:46
  80.1 38.8 %collective-permute-start.2 = (bf16[2,128,48,128]{3,1,0,2:T(8,128)(2,1)}, bf16[2,128,48,128]{3,1,0,2:T(8,128)(2,1)S(1)}, u32[]{:S(2)}, u32[]{:S(2)}) collective-permute-start(bf16[2,128,48,128]{3,1,0,2:T(8,128)(2,1)} %collective-permute-done.1), channel_id=1, source_target_pairs={{0,16},{16,32},{32,48},{48,64},{64,80},{80,96},{96,112},{112,128},... | collective-permute-start | bytes 9437192 | tf_op jit(solution)/shard_map/ppermute | solution.py:22
  125.2 9.4 %copy-start = (s32[16]{0:T(128)S(1)}, s32[16]{0:T(128)}, u32[]{:S(2)}) copy-start(s32[16]{0:T(128)} %param.17) | copy-start | bytes 196
  125.2 10.4 %copy-start.5 = (s32[1,16,12]{1,0,2:T(1,128)S(1)}, s32[1,16,12]{1,0,2:T(1,128)}, u32[]{:S(2)}) copy-start(s32[1,16,12]{1,0,2:T(1,128)} %param.15) | copy-start | bytes 2308
  129.6 146.4 %all-to-all-start = ((bf16[3,2,128,48,128]{4,2,1,0,3:T(8,128)(2,1)}), bf16[3,2,128,48,128]{4,2,1,0,3:T(8,128)(2,1)}, u32[]{:S(2)}, u32[]{:S(2)}) async-start(bf16[3,2,128,48,128]{4,2,1,0,3:T(8,128)(2,1)} %pad_maximum_fusion), calls=%async_computation | async-start | bytes 18874368 | tf_op jit(solution)/shard_map/all_to_all | solution.py:50
  301.4 3.1 copy-start.6
